TPU v7x, 32 devices: a whole 2x2x4 slice. The times are simulated.
32 devices in a mesh: dp: 8 (over y, x, core), tensor: 4 (over z).
Axes of the slice: x: 2, y: 2, z: 4, core: 2. Of those that a mesh axis runs over, the one named last changes fastest.
Arguments:
- latent_in: bfloat16 [16, 256, 768], P('dp', 'tensor'), may hold values from -6 to 6
- condition: bfloat16 [16, 768], P('dp'), may hold values from -6 to 6
- w_ada: bfloat16 [768, 4608], P('dp', 'tensor'), may hold values from -0.21875 to 0.21875
- w_qkv: bfloat16 [3, 768, 768], P(None, 'dp', 'tensor'), may hold values from -0.21875 to 0.21875
- w_proj: bfloat16 [768, 768], P('tensor', 'dp'), may hold values from -1.25 to 1.25
- w_up: bfloat16 [768, 3072], P('dp', 'tensor'), may hold values from -0.21875 to 0.21875
- w_down: bfloat16 [3072, 768], P('tensor', 'dp'), may hold values from -0.109375 to 0.109375
- out_grad: bfloat16 [16, 256, 768], P('dp', 'tensor'), may hold values from -6 to 6
Outputs:
- latent_out: bfloat16 [16, 256, 768], P('dp', 'tensor')
- grad_latent: float32 [16, 256, 768], P('dp', 'tensor')
- grad_condition: float32 [16, 768], P('dp')
- grad_ada: float32 [768, 4608], P('dp', 'tensor')
- grad_qkv: float32 [3, 768, 768], P(None, 'dp', 'tensor')
- grad_proj: float32 [768, 768], P('tensor', 'dp')
- grad_up: float32 [768, 3072], P('dp', 'tensor')
- grad_down: float32 [3072, 768], P('tensor', 'dp')
All inputs are finite; a program needn't handle non-finite values.
Results may differ from a plain program's by a relative error of at most 0.015.
The roundings to bfloat16 on the way count: a program that leaves them out, or rounds other values in their place, can miss the bound.
Values may be sent and summed in bfloat16 or wider, within the bound.
A program may use at most 128 MiB of HBM per device.

v0:
```python
import math
import jax
import jax.numpy as jnp
from jax import lax
from jax.sharding import PartitionSpec as P

HEAD_DIM = 64
EPS = 1e-06
f32 = jnp.float32
bf16 = jnp.bfloat16


def silu_value(values):
    return values / (1.0 + jnp.exp(-values))


def gelu_tanh(values):
    return (
        0.5
        * values
        * (
            1.0
            + jnp.tanh(math.sqrt(2.0 / math.pi) * (values + 0.044715 * values * values * values))
        )
    )


def norm_parts(values):
    centered = values - jnp.mean(values, axis=-1, keepdims=True)
    variance = jnp.mean(centered * centered, axis=-1, keepdims=True)
    inverse = lax.rsqrt(variance + EPS)
    return (centered * inverse, inverse)


def norm_back(normed, inverse, grad):
    return inverse * (
        grad
        - jnp.mean(grad, axis=-1, keepdims=True)
        - normed * jnp.mean(grad * normed, axis=-1, keepdims=True)
    )


def dot(form, left, right):
    return jnp.einsum(form, left, right, preferred_element_type=f32)


def gather_tensor(block, axis):
    return lax.all_gather(block, "tensor", axis=axis, tiled=True)


def reduce_tensor(part):
    return lax.psum(part.astype(bf16), "tensor").astype(f32)


def scatter_tensor(part):
    return lax.psum_scatter(part.astype(bf16), "tensor", scatter_dimension=1, tiled=True).astype(
        f32
    )


def gather_weights(shard):
    return lax.all_gather(shard, "dp", axis=0, tiled=True)


def scatter_grads(grads):
    return lax.psum_scatter(grads.astype(bf16), "dp", scatter_dimension=0, tiled=True).astype(f32)


def modulation_of(cond_mine, w_ada):
    part = jnp.dot(cond_mine, w_ada, preferred_element_type=f32)
    own = lax.psum_scatter(part, "dp", scatter_dimension=0, tiled=True)
    return lax.all_gather(own, "tensor", axis=1, tiled=True)


def shards(latent_in, condition, w_ada, w_qkv, w_proj, w_up, w_down, out_grad):
    rows, own_tokens, width = latent_in.shape
    scale = HEAD_DIM ** (-0.5)
    dp_at = lax.axis_index("dp")
    tensor_at = lax.axis_index("tensor")
    shard_rows = w_ada.shape[0]
    local = w_proj.shape[0]
    heads = local // HEAD_DIM
    units = w_down.shape[0]
    attn_shard = jnp.concatenate([w_qkv[0], w_qkv[1], w_qkv[2], w_proj.T], axis=1)
    ffn_shard = jnp.concatenate([w_up, w_down.T], axis=1)
    cond_all = lax.all_gather(condition, "dp", axis=0, tiled=True)
    cond_act = silu_value(cond_all.astype(f32)).astype(bf16)
    cond_mine = lax.dynamic_slice_in_dim(cond_act, dp_at * shard_rows, shard_rows, 1)
    modulation = modulation_of(cond_mine, w_ada).reshape(rows, 6, 1, width)
    shift_a, scale_a, gate_a, shift_f, scale_f, gate_f = (modulation[:, i] for i in range(6))
    attn_weights = gather_weights(attn_shard)
    w_in = attn_weights[:, : 3 * local]
    proj_t = attn_weights[:, 3 * local :]
    both = gather_tensor(jnp.stack([latent_in, out_grad], axis=0), 2)
    ffn_weights = gather_weights(ffn_shard)
    up = ffn_weights[:, :units]
    down_t = ffn_weights[:, units:]
    tokens = both[0].astype(f32)
    cotangent = both[1].astype(f32)
    seq = tokens.shape[1]
    normed_a, inverse_a = norm_parts(tokens)
    attn_in = (normed_a * (1.0 + scale_a) + shift_a).astype(bf16)
    projected = dot("lsd,de->lse", attn_in, w_in).astype(bf16)
    projected = projected.reshape(rows, seq, 3, heads, HEAD_DIM)
    queries, keys, values = (projected[:, :, 0], projected[:, :, 1], projected[:, :, 2])
    scores = dot("lqhe,lkhe->lhqk", queries, keys) * scale
    shifted = jnp.exp(scores - jnp.max(scores, axis=-1, keepdims=True))
    probs = shifted / jnp.sum(shifted, axis=-1, keepdims=True)
    probs_low = probs.astype(bf16)
    mixed = dot("lhqk,lkhe->lqhe", probs_low, values).reshape(rows, seq, local).astype(bf16)
    attn_out = reduce_tensor(dot("lsd,ed->lse", mixed, proj_t))
    resid = tokens + gate_a * attn_out
    normed_f, inverse_f = norm_parts(resid)
    ffn_in = (normed_f * (1.0 + scale_f) + shift_f).astype(bf16)
    hidden_pre = dot("lsd,dn->lsn", ffn_in, up)
    hidden, gelu_pull = jax.vjp(gelu_tanh, hidden_pre)
    hidden = hidden.astype(bf16)
    d_ffn_out = (gate_f * cotangent).astype(bf16)
    d_hidden_pre = gelu_pull(dot("lse,en->lsn", d_ffn_out, down_t))[0].astype(bf16)
    d_ffn_in = reduce_tensor(dot("lsn,dn->lsd", d_hidden_pre, up))
    ffn_part = dot("lsn,en->lse", hidden, down_t)
    d_gate_f = jnp.sum(cotangent * ffn_part, axis=1)
    ffn_own = scatter_tensor(ffn_part)
    first = tensor_at * own_tokens
    resid_own = lax.dynamic_slice_in_dim(resid, first, own_tokens, 1)
    latent_out = (resid_own + gate_f * ffn_own).astype(bf16)
    grad_ffn = jnp.concatenate(
        [dot("lsd,lsn->dn", ffn_in, d_hidden_pre), dot("lse,lsn->en", d_ffn_out, hidden)], axis=1
    )
    grad_ffn = scatter_grads(grad_ffn)
    d_shift_f = jnp.sum(d_ffn_in, axis=1)
    d_scale_f = jnp.sum(d_ffn_in * normed_f, axis=1)
    d_resid = cotangent + norm_back(normed_f, inverse_f, d_ffn_in * (1.0 + scale_f))
    d_gate_a = jnp.sum(d_resid * attn_out, axis=1)
    d_attn_out = (gate_a * d_resid).astype(bf16)
    d_mixed = dot("lse,ed->lsd", d_attn_out, proj_t).astype(bf16)
    d_mixed = d_mixed.reshape(rows, seq, heads, HEAD_DIM)
    d_probs = dot("lqhe,lkhe->lhqk", d_mixed, values)
    d_scores = probs * (d_probs - jnp.sum(d_probs * probs, axis=-1, keepdims=True))
    d_scores = d_scores.astype(bf16)
    d_values = dot("lhqk,lqhe->lkhe", probs_low, d_mixed)
    d_queries = dot("lhqk,lkhe->lqhe", d_scores, keys) * scale
    d_keys = dot("lhqk,lqhe->lkhe", d_scores, queries) * scale
    d_projected = jnp.stack([d_queries, d_keys, d_values], axis=2)
    d_projected = d_projected.reshape(rows, seq, 3 * local).astype(bf16)
    d_attn_part = dot("lse,de->lsd", d_projected, w_in)
    d_attn_own = scatter_tensor(d_attn_part)
    grad_attn = jnp.concatenate(
        [dot("lsd,lse->de", attn_in, d_projected), dot("lse,lsd->ed", d_attn_out, mixed)], axis=1
    )
    grad_attn = scatter_grads(grad_attn)
    own = lambda value: lax.dynamic_slice_in_dim(value, first, own_tokens, 1)
    grad_latent = own(d_resid) + norm_back(
        own(normed_a), own(inverse_a), d_attn_own * (1.0 + scale_a)
    )
    d_shift_a = jnp.sum(d_attn_part, axis=1)
    d_scale_a = jnp.sum(d_attn_part * normed_a, axis=1)
    ones = jnp.where(tensor_at == 0, 1.0, 0.0)
    d_modulation = jnp.concatenate(
        [d_shift_a, d_scale_a, d_gate_a * ones, d_shift_f * ones, d_scale_f * ones, d_gate_f],
        axis=1,
    )
    d_mod_own = lax.psum_scatter(d_modulation, "tensor", scatter_dimension=1, tiled=True)
    d_mod_all = lax.all_gather(d_mod_own.astype(bf16), "dp", axis=0, tiled=True)
    grad_ada = dot("ld,le->de", cond_mine, d_mod_all)
    act_part = dot("le,de->ld", d_mod_all, w_ada)
    act_all = lax.all_gather(act_part, ("dp", "tensor"), axis=0, tiled=False)
    act_all = act_all.reshape(-1, lax.axis_size("tensor"), cond_all.shape[0], shard_rows)
    act_own = lax.dynamic_slice_in_dim(act_all, dp_at * rows, rows, 2)
    d_act = jnp.sum(act_own, axis=1).transpose(1, 0, 2).reshape(rows, width)
    grad_condition = jax.vjp(silu_value, condition.astype(f32))[1](d_act)[0]
    grad_qkv = jnp.stack([grad_attn[:, j * local : (j + 1) * local] for j in range(3)], axis=0)
    grad_proj = grad_attn[:, 3 * local :].T
    grad_up = grad_ffn[:, :units]
    grad_down = grad_ffn[:, units:].T
    return (
        latent_out,
        grad_latent,
        grad_condition,
        grad_ada,
        grad_qkv,
        grad_proj,
        grad_up,
        grad_down,
    )


def solution(mesh):
    return jax.shard_map(
        shards,
        mesh=mesh,
        in_specs=(
            P("dp", "tensor", None),
            P("dp", None),
            P("dp", "tensor"),
            P(None, "dp", "tensor"),
            P("tensor", "dp"),
            P("dp", "tensor"),
            P("tensor", "dp"),
            P("dp", "tensor", None),
        ),
        out_specs=(
            P("dp", "tensor", None),
            P("dp", "tensor", None),
            P("dp", None),
            P("dp", "tensor"),
            P(None, "dp", "tensor"),
            P("tensor", "dp"),
            P("dp", "tensor"),
            P("tensor", "dp"),
        ),
        check_vma=False,
    )
```

profile of v0, /device:TPU:0, one launch (start us, length us, event | category | flops | bytes accessed | tf_op | source)
XLA Modules:
  0.0 402.7 jit_solution(13563695485046258541)
XLA Ops:
  8.1 10.8 %all-gather.1 = bf16[8,2,768]{2,1,0:T(2,128)(2,1)S(1)} all-gather(bf16[1,2,768]{2,1,0:T(2,128)(2,1)} %bitcast.208), channel_id=1, replica_groups=mesh['dp'=8,'tensor'=4] {'dp'}, dimensions={0}, use_global_device_ids=true | all-gather | bytes 27648 | tf_op jit(solution)/shard_map/all_gather | solution.py:86
  18.9 0.9 fusion.57
  19.8 1.8 pad_maximum_fusion.2
  24.0 45.8 %all-reduce.9.cloned.1.call-done = f32[16,1152]{1,0:T(8,128)} async-done(((f32[16,1152]{1,0:T(8,128)}), f32[16,1152]{1,0:T(8,128)}) %all-reduce.9.cloned.1.call-update) | async-done | bytes 73744
  70.5 13.2 %all_gather.26 = f32[2,4608]{1,0:T(2,128)S(1)} all-gather(f32[2,1152]{1,0:T(2,128)S(1)} %constant_dynamic-slice_fusion.1), channel_id=1, replica_groups=mesh['dp'=8,'tensor'=4] {'tensor'}, dimensions={1}, use_global_device_ids=true | all-gather | bytes 46080 | tf_op jit(solution)/shard_map/all_gather | solution.py:72
  83.9 1.4 convert_reduce_fusion.1
  85.3 1.5 fusion.9
  86.9 2.9 convolution_convert_fusion.2
  89.8 1.7 fusion.62
  92.1 1.2 convolution_convert_fusion.4
  94.0 2.5 convolution_convert_fusion.1
  97.4 43.9 %all-reduce.5.cloned.1.call-done = bf16[2,256,768]{2,1,0:T(8,128)(2,1)} async-done(((bf16[2,256,768]{2,1,0:T(8,128)(2,1)}), bf16[2,256,768]{2,1,0:T(8,128)(2,1)}) %all-reduce.5.cloned.1.call-update) | async-done | bytes 786448 | tf_op jit(solution)/shard_map/psum | solution.py:52
  141.3 1.5 fusion.59
  143.2 2.4 fusion.31
  145.5 1.8 fusion.17
  147.3 0.9 copy-done.32
  148.2 1.7 convolution_convert_fusion
  150.2 42.8 %all-reduce.7.cloned.1.call-done = bf16[2,256,768]{2,1,0:T(8,128)(2,1)} async-done(((bf16[2,256,768]{2,1,0:T(8,128)(2,1)}), bf16[2,256,768]{2,1,0:T(8,128)(2,1)}) %all-reduce.7.cloned.1.call-update) | async-done | bytes 786448 | tf_op jit(solution)/shard_map/psum | solution.py:52
  193.0 2.0 fusion.24
  195.0 2.3 fusion.10
  197.9 0.8 copy-done.9
  201.3 0.9 copy-done.7
  202.1 0.8 fusion.41
  203.9 2.6 fusion.26
  206.5 2.1 copy.86
  210.1 1.4 fusion.28
  211.6 1.9 bitcast_convert_fusion.2
  213.5 1.1 pad_maximum_fusion.1
  214.6 2.4 copy.88
  217.1 2.3 bitcast_convert_fusion.1
  219.4 1.1 bitcast_convert_fusion
  220.5 1.6 pad_maximum_fusion
  222.1 4.3 %copy.90 = bf16[768,1536]{1,0:T(8,128)(2,1)} copy(bf16[768,1536]{0,1:T(8,128)(2,1)} %pad_maximum_fusion) | data formatting | bytes 4718592
  226.5 29.4 %reduce-scatter.16.cloned.1.call-done = f32[1152,2]{1,0:T(8,128)} async-done(((f32[4608,2]{1,0:T(8,128)}), f32[1152,2]{1,0:T(8,128)}) %reduce-scatter.16.cloned.1.call-update) | async-done | bytes 9232
  255.9 1.3 copy.87
  257.2 9.1 %all-gather.2 = bf16[8,2,1152]{2,1,0:T(2,128)(2,1)S(1)} all-gather(bf16[1,2,1152]{2,1,0:T(2,128)(2,1)S(1)} %bitcast.207), channel_id=1, replica_groups=mesh['dp'=8,'tensor'=4] {'dp'}, dimensions={0}, use_global_device_ids=true | all-gather | bytes 41472 | tf_op jit(solution)/shard_map/all_gather | solution.py:164
  266.4 69.4 %all-gather = f32[512,96]{1,0:T(8,128)S(1)} all-gather(f32[16,96]{1,0:T(8,128)S(1)} %fusion.63), channel_id=2, replica_groups=mesh['dp'=8,'tensor'=4] {'dp','tensor'}, dimensions={0}, use_global_device_ids=true | all-gather | bytes 202752 | tf_op jit(solution)/shard_map/all_gather | solution.py:167
  336.6 1.8 fusion.58
  338.4 1.2 fusion.45
  339.7 1.7 add_convert_fusion.3
  341.3 2.0 multiply_add_fusion.2
  343.4 3.1 reduce-scatter.18.cloned.1.call-done
  346.5 1.1 copy.89
  348.3 0.9 copy.77
  349.1 42.9 %reduce-scatter.20.cloned.1.call-done = bf16[96,1536]{1,0:T(8,128)(2,1)} async-done(((bf16[768,1536]{1,0:T(8,128)(2,1)}), bf16[96,1536]{1,0:T(8,128)(2,1)}) %reduce-scatter.20.cloned.1.call-update) | async-done | bytes 294928
  392.0 1.2 copy.91
  393.3 0.9 copy.78
  394.2 0.9 copy.79
  (140 shorter events, 12.8 us)
Async XLA Ops:
  8.0 10.9 %copy-start = (bf16[96,1152]{1,0:T(8,128)(2,1)S(1)}, bf16[96,1152]{1,0:T(8,128)(2,1)}, u32[]{:S(2)}) copy-start(bf16[96,1152]{1,0:T(8,128)(2,1)} %param.10) | copy-start | bytes 663556
  8.0 14.7 %copy-start.28 = (u32[32]{0:T(128)S(1)}, u32[32]{0:T(128)}, u32[]{:S(2)}) copy-start(u32[32]{0:T(128)} %constant.60) | copy-start | bytes 388
  8.0 13.7 %copy-start.16 = (bf16[192,96]{1,0:T(8,128)(2,1)S(1)}, bf16[192,96]{1,0:T(8,128)(2,1)}, u32[]{:S(2)}) copy-start(bf16[192,96]{1,0:T(8,128)(2,1)} %param.12) | copy-start | bytes 110596
  8.0 13.8 %copy-start.12 = (bf16[3,96,192]{2,1,0:T(8,128)(2,1)S(1)}, bf16[3,96,192]{2,1,0:T(8,128)(2,1)}, u32[]{:S(2)}) copy-start(bf16[3,96,192]{2,1,0:T(8,128)(2,1)} %param.11) | copy-start | bytes 331780
  8.0 61.7 %all-reduce.9.cloned.1.call-start = ((), (), s32[]{:S(2)}) async-start(), calls=%async_computation.15 | async-start | bytes 147456
  18.9 66.4 %copy-start.15 = (f32[16,768]{1,0:T(8,128)}, f32[16,768]{1,0:T(8,128)S(1)}, u32[]{:S(2)}) copy-start(f32[16,768]{1,0:T(8,128)S(1)} %reshape.138) | copy-start | bytes 147460
  19.8 64.1 %all-gather.7.cloned.1.call-start = ((), (), s32[]{:S(2)}) async-start(), calls=%async_computation.5 | async-start | bytes 1966080 | tf_op jit(solution)/shard_map/all_gather | solution.py:48
  21.7 65.2 %all-gather.9.cloned.1.call-start = ((), (), s32[]{:S(2)}) async-start(), calls=%async_computation.6 | async-start | bytes 1327104 | tf_op jit(solution)/shard_map/all_gather | solution.py:62
  22.7 118.6 %all-reduce.5.cloned.1.call-start = ((), (), s32[]{:S(2)}) async-start(), calls=%async_computation.7 | async-start | bytes 1572864 | tf_op jit(solution)/shard_map/psum | solution.py:52
  83.8 6.0 %copy-start.22 = (f32[2,1,1,768]{3,0,1,2:T(2,128)}, f32[2,1,1,768]{3,0,1,2:T(2,128)S(1)}, u32[]{:S(2)}) copy-start(f32[2,1,1,768]{3,0,1,2:T(2,128)S(1)} %copy.110) | copy-start | bytes 18436
  83.9 3.0 copy-start.1
  85.3 4.5 %copy-start.20 = (f32[2,256]{1,0:T(2,128)}, f32[2,256]{1,0:T(2,128)S(1)}, u32[]{:S(2)}) copy-start(f32[2,256]{1,0:T(2,128)S(1)} %broadcast_multiply_fusion.3) | copy-start | bytes 6148
  86.9 2.9 copy-start.24
  91.5 0.6 copy-start.18
  91.5 1.8 copy-start.8
  93.3 0.7 copy-start.10
  93.3 3.2 copy-start.13
  94.0 2.6 copy-start.14
  96.5 46.6 %all-gather.11.cloned.1.call-start = ((), (), s32[]{:S(2)}) async-start(), calls=%async_computation.8 | async-start | bytes 2654208 | tf_op jit(solution)/shard_map/all_gather | solution.py:62
  97.3 95.6 %all-reduce.7.cloned.1.call-start = ((), (), s32[]{:S(2)}) async-start(), calls=%async_computation.10 | async-start | bytes 1572864 | tf_op jit(solution)/shard_map/psum | solution.py:52
  143.1 2.4 copy-start.26
  145.5 1.8 copy-start.29
  147.3 0.9 copy-start.32
  149.9 106.0 %reduce-scatter.16.cloned.1.call-start = ((), (), s32[]{:S(2)}) async-start(), calls=%async_computation.12 | async-start | bytes 2949120
  193.0 2.0 copy-start.5
  195.0 2.4 copy-start.6
  197.3 1.4 copy-start.9
  197.3 1.4 copy-start.19
  198.8 1.1 copy-start.11
  200.9 2.1 copy-start.30
  201.2 2.1 copy-start.27
  201.3 0.9 copy-start.7
  202.1 1.7 copy-start.2
  202.1 1.7 copy-start.21
  202.1 1.7 copy-start.25
  208.7 129.7 %reduce-scatter.14.cloned.1.call-start = ((), (), s32[]{:S(2)}) async-start(), calls=%async_computation.11 | async-start | bytes 983040 | tf_op jit(solution)/shard_map/reduce_scatter | solution.py:56
  209.4 2.1 copy-start.23
  209.4 130.2 %reduce-scatter.12.cloned.1.call-start = ((), (), s32[]{:S(2)}) async-start(), calls=%async_computation.9 | async-start | bytes 983040 | tf_op jit(solution)/shard_map/reduce_scatter | solution.py:56
  210.0 136.4 %reduce-scatter.18.cloned.1.call-start = ((), (), s32[]{:S(2)}) async-start(), calls=%async_computation.13 | async-start | bytes 1327104
  210.1 1.5 copy-start.3
  217.1 175.0 %reduce-scatter.20.cloned.1.call-start = ((), (), s32[]{:S(2)}) async-start(), calls=%async_computation.14 | async-start | bytes 2654208
  217.1 2.3 copy-start.4
  217.1 2.3 copy-start.31
  226.4 109.6 %copy-start.17 = (bf16[2,768]{1,0:T(2,128)(2,1)S(1)}, bf16[2,768]{1,0:T(2,128)(2,1)}, u32[]{:S(2)}) copy-start(bf16[2,768]{1,0:T(2,128)(2,1)} %param.9) | copy-start | bytes 9220
Sparse Core Ops, SparseCore 0:
  19.9 49.8 all-reduce.8
  100.0 30.1 all-gather.10
Sparse Core Ops, SparseCore 1:
  22.4 37.1 all-gather.6
  61.9 22.7 all-gather.8
  96.6 44.7 all-reduce.4
  150.0 42.9 all-reduce.6
  208.8 47.1 reduce-scatter.15
  258.3 23.4 reduce-scatter.13
  284.1 23.1 reduce-scatter.11
  310.7 35.7 reduce-scatter.17
  349.7 42.3 reduce-scatter.19
where the time goes:
time: 404 us; the launch traced here: 403 us
  waiting for transfers between devices  209 us (52%)
  blocking collectives  102 us (25%)
  matrix products  28.9 us (7%)
  local copies, waits for them, and re-layouts  23 us (6%)
  other arithmetic  21.2 us (5%)
  between operations  17.1 us (4%)
    unnamed x15, waiting for transfers between devices  123 us
    psum x2, waiting for transfers between devices, reduce_tensor(): return lax.psum(part.astype(bf16), 'tensor').astype(f32)  86.7 us
    all_gather x1, blocking collectives, shards(): act_all = lax.all_gather(act_part, ('dp', 'tensor'), axis=0, tiled=False)  69.4 us
    dot_general x19, matrix products, dot(): return jnp.einsum(form, left, right, preferred_element_type=f32)  26.4 us
    unnamed x86, local copies, waits for them, and re-layouts  22 us
    all_gather x1, blocking collectives, modulation_of(): return lax.all_gather(own, 'tensor', axis=1, tiled=True)  13.2 us
    all_gather x1, blocking collectives, shards(): cond_all = lax.all_gather(condition, 'dp', axis=0, tiled=True)  10.8 us
    all_gather x1, blocking collectives, shards(): d_mod_all = lax.all_gather(d_mod_own.astype(bf16), 'dp', axis=0, tiled=True)  9.06 us
  transfers between devices with their start and end apart: 11, of which 6 were waited for; matrix products, arithmetic and copies ran while one was open for 9% of the time, Pallas kernels for 0%

commit v1 on v0

--- a/solution.py
+++ b/solution.py
@@ -49,7 +49,7 @@
 
 
 def reduce_tensor(part):
-    return lax.psum(part.astype(bf16), "tensor").astype(f32)
+    return jnp.sum(lax.all_gather(part.astype(bf16), "tensor"), axis=0).astype(f32)
 
 
 def scatter_tensor(part):

time: 404 us -> 425 us (1.052)
  waiting for transfers between devices: 209 us -> 223 us
  local copies, waits for them, and re-layouts: 23 us -> 29.2 us
  other arithmetic: 21.2 us -> 26.3 us
    all_gather x0 -> x2, waiting for transfers between devices: none -> 117 us  [reduce_tensor(): lax.all_gather(part.astype(bf16), 'tensor')]
    psum x2 -> x0, waiting for transfers between devices: 86.7 us -> none  [reduce_tensor(): return lax.psum(part.astype(bf16), 'tensor').astype(f32)]
    unnamed x15, waiting for transfers between devices: 123 us -> 79.9 us
    all_gather x2, waiting for transfers between devices: 0.05 us -> 25.5 us  [gather_weights(): return lax.all_gather(shard, 'dp', axis=0, tiled=True)]
    reduce_sum x0 -> x2, other arithmetic: none -> 5.21 us  [reduce_tensor(): jnp.sum(lax.all_gather(part.astype(bf16), 'tensor'), axis=0).astype(f32)]
    unnamed x86 -> x80, local copies, waits for them, and re-layouts: 22 us -> 25.7 us
  transfers between devices with their start and end apart: 11 -> 11, of which waited for: 6 -> 6; matrix products, arithmetic and copies ran while one was open for 9% -> 14% of each run, Pallas kernels for 0% -> 0%
where the time goes in v1:
time: 425 us; the launch traced here: 424 us
  waiting for transfers between devices  223 us (52%)
  blocking collectives  103 us (24%)
  local copies, waits for them, and re-layouts  29.2 us (7%)
  other arithmetic  26.3 us (6%)
  matrix products  25.6 us (6%)
  between operations  17 us (4%)
    all_gather x2, waiting for transfers between devices, reduce_tensor(): lax.all_gather(part.astype(bf16), 'tensor')  117 us
    unnamed x15, waiting for transfers between devices  79.9 us
    all_gather x1, blocking collectives, shards(): act_all = lax.all_gather(act_part, ('dp', 'tensor'), axis=0, tiled=False)  69.6 us
    unnamed x80, local copies, waits for them, and re-layouts  25.7 us
    all_gather x2, waiting for transfers between devices, gather_weights(): return lax.all_gather(shard, 'dp', axis=0, tiled=True)  25.5 us
    dot_general x19, matrix products, dot(): return jnp.einsum(form, left, right, preferred_element_type=f32)  24 us
    all_gather x1, blocking collectives, modulation_of(): return lax.all_gather(own, 'tensor', axis=1, tiled=True)  13.2 us
    all_gather x1, blocking collectives, shards(): cond_all = lax.all_gather(condition, 'dp', axis=0, tiled=True)  10.8 us
  transfers between devices with their start and end apart: 11, of which 6 were waited for; matrix products, arithmetic and copies ran while one was open for 14% of the time, Pallas kernels for 0%

profile of v1, /device:TPU:0, one launch (start us, length us, event | category | flops | bytes accessed | tf_op | source)
XLA Modules:
  0.0 424.2 jit_solution(17461358814347903465)
XLA Ops:
  8.1 10.8 %all-gather.3 = bf16[8,2,768]{2,1,0:T(2,128)(2,1)S(1)} all-gather(bf16[1,2,768]{2,1,0:T(2,128)(2,1)} %bitcast.248), channel_id=1, replica_groups=mesh['dp'=8,'tensor'=4] {'dp'}, dimensions={0}, use_global_device_ids=true | all-gather | bytes 27648 | tf_op jit(solution)/shard_map/all_gather | solution.py:86
  18.9 0.9 fusion.78
  19.8 1.8 pad_maximum_fusion.2
  24.0 45.8 %all-reduce.3.cloned.1.call-done = f32[16,1152]{1,0:T(8,128)} async-done(((f32[16,1152]{1,0:T(8,128)}), f32[16,1152]{1,0:T(8,128)}) %all-reduce.3.cloned.1.call-update) | async-done | bytes 73744
  70.5 13.2 %all_gather.38 = f32[2,4608]{1,0:T(2,128)S(1)} all-gather(f32[2,1152]{1,0:T(2,128)S(1)} %constant_dynamic-slice_fusion.1), channel_id=1, replica_groups=mesh['dp'=8,'tensor'=4] {'tensor'}, dimensions={1}, use_global_device_ids=true | all-gather | bytes 46080 | tf_op jit(solution)/shard_map/all_gather | solution.py:72
  83.9 1.4 convert_reduce_fusion.1
  85.3 1.5 fusion.12
  86.9 2.0 convolution_convert_fusion.2
  89.9 1.0 copy-done.12
  91.5 2.4 convolution_convert_fusion.1
  94.9 63.6 %all-gather.17.cloned.1.call-done = bf16[8,256,768]{2,1,0:T(8,128)(2,1)} async-done(((bf16[2,256,768]{2,1,0:T(8,128)(2,1)}), bf16[8,256,768]{2,1,0:T(8,128)(2,1)}) %all-gather.17.cloned.1.call-update) | async-done | bytes 3145744 | tf_op jit(solution)/shard_map/all_gather | solution.py:52
  158.5 2.6 reduce_sum.180
  161.1 1.8 fusion.81
  163.2 25.4 %all-gather.15.cloned.1.call-done = bf16[768,1536]{1,0:T(8,128)(2,1)} async-done(((bf16[96,1536]{1,0:T(8,128)(2,1)}), bf16[768,1536]{1,0:T(8,128)(2,1)}) %all-gather.15.cloned.1.call-update) | async-done | bytes 2359312 | tf_op jit(solution)/shard_map/all_gather | solution.py:62
  188.7 2.4 fusion.44
  191.2 1.8 fusion.23
  193.0 0.9 copy-done.29
  193.9 1.7 convolution_convert_fusion
  195.7 2.2 bitcast_convert_fusion.1
  197.9 1.1 bitcast_convert_fusion
  199.0 1.6 pad_maximum_fusion
  200.6 4.3 %copy.90 = bf16[768,1536]{1,0:T(8,128)(2,1)} copy(bf16[768,1536]{0,1:T(8,128)(2,1)} %pad_maximum_fusion) | data formatting | bytes 4718592
  205.2 53.9 %all-gather.19.cloned.1.call-done = bf16[8,256,768]{2,1,0:T(8,128)(2,1)} async-done(((bf16[2,256,768]{2,1,0:T(8,128)(2,1)}), bf16[8,256,768]{2,1,0:T(8,128)(2,1)}) %all-gather.19.cloned.1.call-update) | async-done | bytes 3145744 | tf_op jit(solution)/shard_map/all_gather | solution.py:52
  259.1 2.6 reduce_sum.183
  263.6 2.1 fusion.24
  270.8 0.9 copy-done.24
  271.7 2.6 fusion.14
  274.5 2.1 copy.86
  277.9 1.9 copy.91
  279.8 1.0 convert_element_type.198
  280.9 1.8 slice.115
  283.4 1.9 copy.79
  285.3 1.9 copy.78
  287.1 2.3 bitcast_convert_fusion.2
  289.5 1.1 fusion.41
  290.6 1.1 pad_maximum_fusion.1
  291.7 2.4 copy.88
  294.1 29.4 %reduce-scatter.16.cloned.1.call-done = f32[1152,2]{1,0:T(8,128)} async-done(((f32[4608,2]{1,0:T(8,128)}), f32[1152,2]{1,0:T(8,128)}) %reduce-scatter.16.cloned.1.call-update) | async-done | bytes 9232
  323.5 1.3 copy.87
  324.7 9.1 %all-gather.4 = bf16[8,2,1152]{2,1,0:T(2,128)(2,1)S(1)} all-gather(bf16[1,2,1152]{2,1,0:T(2,128)(2,1)S(1)} %bitcast.247), channel_id=1, replica_groups=mesh['dp'=8,'tensor'=4] {'dp'}, dimensions={0}, use_global_device_ids=true | all-gather | bytes 41472 | tf_op jit(solution)/shard_map/all_gather | solution.py:164
  334.0 69.6 %all-gather.2 = f32[512,96]{1,0:T(8,128)S(1)} all-gather(f32[16,96]{1,0:T(8,128)S(1)} %fusion.85), channel_id=4, replica_groups=mesh['dp'=8,'tensor'=4] {'dp','tensor'}, dimensions={0}, use_global_device_ids=true | all-gather | bytes 202752 | tf_op jit(solution)/shard_map/all_gather | solution.py:167
  404.3 1.1 fusion.79
  405.4 1.2 fusion.64
  406.7 1.7 add_convert_fusion.3
  408.3 2.1 multiply_add_fusion.2
  410.4 3.5 reduce-scatter.18.cloned.1.call-done
  413.9 1.1 copy.89
  415.7 0.9 copy.77
  (136 shorter events, 16.6 us)
Async XLA Ops:
  8.0 10.9 %copy-start = (bf16[96,1152]{1,0:T(8,128)(2,1)S(1)}, bf16[96,1152]{1,0:T(8,128)(2,1)}, u32[]{:S(2)}) copy-start(bf16[96,1152]{1,0:T(8,128)(2,1)} %param.10) | copy-start | bytes 663556
  8.0 14.7 %copy-start.25 = (u32[32]{0:T(128)S(1)}, u32[32]{0:T(128)}, u32[]{:S(2)}) copy-start(u32[32]{0:T(128)} %constant.63) | copy-start | bytes 388
  8.0 13.7 %copy-start.21 = (bf16[192,96]{1,0:T(8,128)(2,1)S(1)}, bf16[192,96]{1,0:T(8,128)(2,1)}, u32[]{:S(2)}) copy-start(bf16[192,96]{1,0:T(8,128)(2,1)} %param.12) | copy-start | bytes 110596
  8.0 13.8 %copy-start.18 = (bf16[3,96,192]{2,1,0:T(8,128)(2,1)S(1)}, bf16[3,96,192]{2,1,0:T(8,128)(2,1)}, u32[]{:S(2)}) copy-start(bf16[3,96,192]{2,1,0:T(8,128)(2,1)} %param.11) | copy-start | bytes 331780
  8.0 61.7 %all-reduce.3.cloned.1.call-start = ((), (), s32[]{:S(2)}) async-start(), calls=%async_computation.15 | async-start | bytes 147456
  19.8 64.1 %all-gather.11.cloned.1.call-start = ((), (), s32[]{:S(2)}) async-start(), calls=%async_computation.5 | async-start | bytes 1966080 | tf_op jit(solution)/shard_map/all_gather | solution.py:48
  21.7 65.2 %all-gather.13.cloned.1.call-start = ((), (), s32[]{:S(2)}) async-start(), calls=%async_computation.6 | async-start | bytes 1327104 | tf_op jit(solution)/shard_map/all_gather | solution.py:62
  22.7 135.8 %all-gather.17.cloned.1.call-start = ((), (), s32[]{:S(2)}) async-start(), calls=%async_computation.10 | async-start | bytes 3932160 | tf_op jit(solution)/shard_map/all_gather | solution.py:52
  83.9 3.0 copy-start.6
  88.9 1.0 copy-start.14
  89.6 1.2 copy-start.12
  90.9 0.7 copy-start.16
  90.9 3.2 copy-start.19
  90.9 3.2 copy-start.20
  94.0 94.7 %all-gather.15.cloned.1.call-start = ((), (), s32[]{:S(2)}) async-start(), calls=%async_computation.7 | async-start | bytes 2654208 | tf_op jit(solution)/shard_map/all_gather | solution.py:62
  94.8 164.2 %all-gather.19.cloned.1.call-start = ((), (), s32[]{:S(2)}) async-start(), calls=%async_computation.11 | async-start | bytes 3932160 | tf_op jit(solution)/shard_map/all_gather | solution.py:52
  161.1 1.8 copy-start.1
  188.7 2.4 copy-start.7
  188.7 2.5 copy-start.23
  191.0 1.9 copy-start.26
  192.9 0.9 copy-start.29
  195.6 82.3 %reduce-scatter.20.cloned.1.call-start = ((), (), s32[]{:S(2)}) async-start(), calls=%async_computation.14 | async-start | bytes 2654208
  195.7 2.2 copy-start.27
  205.0 118.5 %reduce-scatter.16.cloned.1.call-start = ((), (), s32[]{:S(2)}) async-start(), calls=%async_computation.12 | async-start | bytes 2949120
  261.7 0.9 copy-start.4
  261.7 1.4 copy-start.2
  261.7 1.9 copy-start.8
  263.6 2.1 copy-start.10
  265.7 1.4 copy-start.13
  265.7 1.5 copy-start.15
  269.1 1.7 copy-start.28
  269.1 0.8 copy-start.11
  270.0 1.8 copy-start.24
  276.6 128.8 %reduce-scatter.14.cloned.1.call-start = ((), (), s32[]{:S(2)}) async-start(), calls=%async_computation.9 | async-start | bytes 983040 | tf_op jit(solution)/shard_map/reduce_scatter | solution.py:56
  277.2 129.5 %reduce-scatter.12.cloned.1.call-start = ((), (), s32[]{:S(2)}) async-start(), calls=%async_computation.8 | async-start | bytes 983040 | tf_op jit(solution)/shard_map/reduce_scatter | solution.py:56
  277.8 136.1 %reduce-scatter.18.cloned.1.call-start = ((), (), s32[]{:S(2)}) async-start(), calls=%async_computation.13 | async-start | bytes 1327104
  287.1 2.3 copy-start.3
  287.1 2.3 copy-start.5
  287.1 2.4 copy-start.9
  287.1 2.4 copy-start.17
  294.1 109.6 %copy-start.22 = (bf16[2,768]{1,0:T(2,128)(2,1)S(1)}, bf16[2,768]{1,0:T(2,128)(2,1)}, u32[]{:S(2)}) copy-start(bf16[2,768]{1,0:T(2,128)(2,1)} %param.9) | copy-start | bytes 9220
Sparse Core Ops, SparseCore 0:
  19.9 49.8 all-reduce.2
  205.1 42.4 reduce-scatter.19
  276.7 46.6 reduce-scatter.15
  325.6 23.4 reduce-scatter.13
  351.3 23.5 reduce-scatter.11
  377.9 35.9 reduce-scatter.17
Sparse Core Ops, SparseCore 1:
  22.5 37.1 all-gather.10
  62.1 22.7 all-gather.12
  94.1 64.4 all-gather.16
  161.1 27.5 all-gather.14
  195.7 63.3 all-gather.18
